TPU v7x, 256 devices: a whole 4x4x8 slice. The times are simulated.
256 devices in a mesh: layer: 16 (over z_lo, y), lat: 16 (over z_hi, x, core).
Axes of the slice: x: 4, y: 4, z: 8 (z_hi: 2, z_lo: 4; z = z_hi * 4 + z_lo), core: 2. Of those that a mesh axis runs over, the one named last changes fastest.
Arguments:
- inputs: bfloat16 [128, 4, 2048], P(None, None, 'layer'), may hold values from -6 to 6
- encoder: bfloat16 [4, 2048, 16384], P(None, 'layer', 'lat'), may hold values from -0.125 to 0.125
- enc_bias: float32 [4, 16384], P(None, 'lat'), may hold values from -3 to 3
- decoder: bfloat16 [16, 5, 16384, 256], P('layer', None, 'lat'), may hold values from -0.375 to 0.375
- dec_bias: float32 [16, 2, 256], P('layer'), may hold values from -3 to 3
- targets: bfloat16 [16, 128, 2, 256], P('layer'), may hold values from -6 to 6
- top_index: int32 [128, 4, 64], replicated, may hold values from 0 to 16383, as said below
Outputs:
- decoder_grad: float32 [16, 5, 16384, 256], P('layer', None, 'lat')
- encoder_grad: float32 [4, 2048, 16384], P(None, 'layer', 'lat')
- bias_grad: float32 [4, 16384], P(None, 'lat')
Inputs may be any that keep to these rules, and one draw needn't show every extreme that they name: `top_index`: the 64 entries of one token and layer are distinct; at most 8 of them have the same value of n // 1024, and every value of n // 1024 is taken by exactly 8 entries of some token and layer.
All inputs are finite; a program needn't handle non-finite values.
Results may differ from a plain program's by a relative error of at most 0.0045.
Values may be sent and summed in bfloat16 or wider, within the bound.
A program may use at most 64 MiB of HBM per device.

v0:
```python
import jax
import jax.numpy as jnp
from jax import lax
from jax.sharding import PartitionSpec as P

FEAT_SPLIT = 8


def pick_rows(weight_table, row_index):
    return jnp.take(weight_table, row_index, axis=0)


def body(inputs, encoder, enc_bias, decoder, dec_bias, targets, top_index):
    tokens, layers, top_count = top_index.shape
    slab_width = encoder.shape[2]
    slab_most = 2 * top_count // lax.axis_size("lat")
    pair_index = lax.axis_index("layer") // FEAT_SPLIT
    slab_index = lax.axis_index("lat")
    blocks = decoder.shape[1]
    decoder_own = decoder[0]
    local_index = top_index - slab_index * slab_width
    inside = (local_index >= 0) & (local_index < slab_width)
    position_ids = lax.broadcasted_iota(jnp.int32, top_index.shape, 2)
    order_key = jnp.where(inside, 2 * top_count, top_count) - position_ids
    slot_key, position = lax.top_k(order_key, slab_most)
    valid_slot = slot_key > top_count
    picked = jnp.take_along_axis(jnp.where(inside, local_index, 0), position, axis=2)
    encoder_rows = jnp.swapaxes(encoder, 1, 2)
    columns = jax.vmap(pick_rows, in_axes=(0, 1), out_axes=1)(encoder_rows, picked)
    partial_value = jnp.einsum("tld,tlsd->tls", inputs, columns, preferred_element_type=jnp.float32)
    pre_total = lax.psum(partial_value, "layer")
    bias_picked = jax.vmap(pick_rows, in_axes=(0, 1), out_axes=1)(enc_bias, picked)
    pre_value = (pre_total + bias_picked).astype(jnp.bfloat16)
    act_slots = lax.optimization_barrier(
        jnp.where(valid_slot, pre_value, jnp.zeros_like(pre_value))
    )
    token_ids = lax.broadcasted_iota(jnp.int32, picked.shape, 0)
    layer_ids = lax.broadcasted_iota(jnp.int32, picked.shape, 1)
    act_dense = (
        jnp.zeros((tokens, layers, slab_width), jnp.bfloat16)
        .at[token_ids, layer_ids, picked]
        .add(act_slots)
    )
    block_ids = jnp.arange(blocks, dtype=jnp.int32)
    first_target = block_ids <= pair_index
    source = jnp.where(first_target, block_ids, block_ids - pair_index - 1)
    slot_ids = jnp.where(first_target, 0, 1).astype(jnp.int32)
    slot_weight = jnp.stack([first_target, jnp.logical_not(first_target)], axis=1).astype(
        jnp.float32
    )
    source_onehot = (source[:, None] == jnp.arange(layers, dtype=jnp.int32)[None, :]).astype(
        jnp.float32
    )
    act_source = jnp.take(act_dense, source, axis=1)
    picked_source = jnp.take(picked, source, axis=1)
    per_block = jnp.einsum(
        "tks,ksf->tkf", act_source, decoder_own, preferred_element_type=jnp.float32
    )
    rebuilt = lax.psum(
        jnp.einsum("tkf,kc->tcf", per_block, slot_weight, precision=lax.Precision.HIGHEST), "lat"
    )
    residue = (rebuilt + dec_bias[0][None, :, :] - targets[0].astype(jnp.float32)).astype(
        jnp.bfloat16
    )
    residue = lax.optimization_barrier(residue)
    residue_block = jnp.take(residue, slot_ids, axis=1)
    block_grad = jnp.einsum(
        "tks,tkf->ksf", act_source, residue_block, preferred_element_type=jnp.float32
    )
    dense_grad = jnp.einsum(
        "tkf,ksf->tks", residue_block, decoder_own, preferred_element_type=jnp.float32
    )
    per_block = jnp.take_along_axis(dense_grad, picked_source, axis=2)
    grad_slots = lax.psum(
        jnp.einsum("tks,kl->tls", per_block, source_onehot, precision=lax.Precision.HIGHEST),
        "layer",
    ).astype(jnp.bfloat16)
    pre_grad = lax.optimization_barrier(
        jnp.where(valid_slot, grad_slots, jnp.zeros_like(grad_slots))
    )
    grad_dense = (
        jnp.zeros((tokens, layers, slab_width), jnp.bfloat16)
        .at[token_ids, layer_ids, picked]
        .add(pre_grad)
    )
    encoder_grad = jnp.einsum(
        "tld,tln->ldn", inputs, grad_dense, preferred_element_type=jnp.float32
    )
    bias_grad = jnp.sum(grad_dense, axis=0, dtype=jnp.float32)
    return (block_grad[None], encoder_grad, bias_grad)


def solution(mesh):
    return jax.shard_map(
        body,
        mesh=mesh,
        in_specs=(
            P(None, None, "layer"),
            P(None, "layer", "lat"),
            P(None, "lat"),
            P("layer", None, "lat", None),
            P("layer", None, None),
            P("layer", None, None, None),
            P(),
        ),
        out_specs=(P("layer", None, "lat", None), P(None, "layer", "lat"), P(None, "lat")),
        check_vma=False,
    )
```

profile of v0, /device:TPU:6, one launch (start us, length us, event | category | flops | bytes accessed | tf_op | source)
XLA Modules:
  0.0 727.5 jit_solution(8316755115968587439)
XLA Ops:
  7.2 0.5 compare_and_fusion.2
  7.8 0.6 iota_compare_fusion.1
  8.4 0.9 iota_subtract_fusion
  9.3 1.7 top_k.12
  11.5 33.2 %gather_fusion.3 = s32[4096]{0:T(1024)S(1)} fusion(s32[128,4,64]{0,2,1:T(8,128)S(1)} %get-tuple-element.26, s32[4096]{0:T(1024)S(1)} %reshape.136), kind=kCustom, calls=%fused_computation.3 | custom fusion | bytes 81920 | tf_op jit(solution)/shard_map/jit(take_along_axis)/gather | solution.py:27
  46.1 34.9 %gather_fusion.5 = f32[4096]{0:T(1024)S(1)} fusion(f32[4,1024]{1,0:T(4,128)S(1)} %copy-done.1, s32[4096]{0:T(1024)S(1)} %reshape.142), kind=kCustom, calls=%fused_computation.5 | custom fusion | bytes 65536 | tf_op jit(solution)/shard_map/vmap(jit(_take))/gather | solution.py:10
  81.7 2.3 copy.62
  84.0 120.8 %gather_fusion.4 = bf16[4096,128]{1,0:T(8,128)(2,1)} fusion(bf16[4,1024,128]{2,1,0:T(8,128)(2,1)} %bitcast.88, s32[4096]{0:T(1024)S(1)} %reshape.142), kind=kCustom, calls=%fused_computation.4 | custom fusion | bytes 2129920 | tf_op jit(solution)/shard_map/vmap(jit(_take))/gather | solution.py:10
  204.9 2.1 fusion.16
  207.1 81.2 %psum.21 = f32[128,4,8]{0,1,2:T(4,128)S(1)} all-reduce(f32[128,4,8]{0,1,2:T(4,128)S(1)} %bitcast.91), channel_id=1, replica_groups=mesh['layer'=16,'lat'=16] {'layer'}, use_global_device_ids=true, to_apply=%region_1.2 | all-reduce | flops 4096 | bytes 32768 | tf_op jit(solution)/shard_map/psum | solution.py:31
  288.3 0.6 fusion.33
  289.2 29.7 %scatter_custom_fusion = bf16[524288]{0:T(1024)(128)(2,1)} fusion(s32[4096]{0:T(1024)S(1)} %reshape.160, bf16[4096]{0:T(1024)(128)(2,1)S(1)} %reshape.162, bf16[]{:T(256)} %constant.131.clone.1), kind=kCustom, calls=%fused_computation.30 | custom fusion | flops 4096 | bytes 1048578
  319.0 2.1 reshape.106
  321.1 2.5 copy.66
  323.6 3.0 gather_fusion
  326.6 1.9 fusion.9
  328.6 1.7 convolution_bitcast_fusion.2
  330.3 0.6 gather_fusion.2
  331.0 0.5 copy-done.2
  332.4 172.4 %all-reduce.2.cloned.1.call-done = f32[128,2,256]{2,1,0:T(2,128)} async-done(((f32[128,2,256]{2,1,0:T(2,128)}), f32[128,2,256]{2,1,0:T(2,128)}) %all-reduce.2.cloned.1.call-update) | async-done | bytes 262160 | tf_op jit(solution)/shard_map/psum | solution.py:59
  504.8 1.1 fusion.24
  505.9 0.6 gather_fusion.1
  506.5 0.7 copy-done.5
  507.2 2.5 fusion.4
  509.7 86.8 %gather_fusion.6 = f32[5120]{0:T(1024)S(1)} fusion(f32[128,5,1024]{2,0,1:T(8,128)} %fusion.4, s32[5120]{0:T(1024)S(1)} %reshape.154), kind=kCustom, calls=%fused_computation.6 | custom fusion | bytes 102400 | tf_op jit(solution)/shard_map/jit(take_along_axis)/gather | solution.py:73
  597.0 79.4 %psum.23 = bf16[128,4,8]{0,1,2:T(4,128)(2,1)S(1)} all-reduce(f32[128,4,8]{0,1,2:T(4,128)S(1)} %convolution_bitcast_fusion.3), channel_id=1, replica_groups=mesh['layer'=16,'lat'=16] {'layer'}, use_global_device_ids=true, to_apply=%region_4.5 | all-reduce | flops 4096 | bytes 24576 | tf_op jit(solution)/shard_map/psum | solution.py:74
  676.8 29.9 %scatter_custom_fusion.1 = bf16[524288]{0:T(1024)(128)(2,1)} fusion(s32[4096]{0:T(1024)} %copy-done.10, bf16[4096]{0:T(1024)(128)(2,1)S(1)} %reshape.168, bf16[]{:T(256)} %constant.131.clone.1), kind=kCustom, calls=%fused_computation.28 | custom fusion | flops 4096 | bytes 1049088
  706.6 2.2 reshape.110
  708.8 2.4 convert_reduce_fusion
  711.2 3.2 convolution_bitcast_fusion.1
  714.5 3.4 convolution_bitcast_fusion
  717.8 2.9 copy.77
  (88 shorter events, 4.8 us)
Async XLA Ops:
  7.2 319.4 %copy-start = (bf16[1,5,1024,256]{3,2,1,0:T(8,128)(2,1)S(1)}, bf16[1,5,1024,256]{3,2,1,0:T(8,128)(2,1)}, u32[]{:S(2)}) copy-start(bf16[1,5,1024,256]{3,2,1,0:T(8,128)(2,1)} %param.10) | copy-start | bytes 7864324
  7.2 497.6 %all-reduce.2.cloned.1.call-start = ((), (), s32[]{:S(2)}) async-start(), calls=%async_computation | async-start | bytes 524288 | tf_op jit(solution)/shard_map/psum | solution.py:59
  11.5 33.9 %copy-start.20 = (s32[3]{0:T(128)S(1)}, s32[3]{0:T(128)}, u32[]{:S(2)}) copy-start(s32[3]{0:T(128)} %constant.147) | copy-start | bytes 40
  11.5 34.0 %copy-start.19 = (s32[3]{0:T(128)S(1)}, s32[3]{0:T(128)}, u32[]{:S(2)}) copy-start(s32[3]{0:T(128)} %constant.144) | copy-start | bytes 40
  44.8 1.4 copy-start.1
  81.7 207.5 %copy-start.10 = (s32[4096]{0:T(1024)}, s32[4096]{0:T(1024)S(1)}, u32[]{:S(2)}) copy-start(s32[4096]{0:T(1024)S(1)} %reshape.160) | copy-start | bytes 49156
  84.0 120.8 %copy-start.7 = (bf16[128,4,128]{2,1,0:T(4,128)(2,1)S(1)}, bf16[128,4,128]{2,1,0:T(4,128)(2,1)}, u32[]{:S(2)}) copy-start(bf16[128,4,128]{2,1,0:T(4,128)(2,1)} %param.7) | copy-start | bytes 393220
  323.6 3.0 copy-start.12
  326.6 2.0 copy-start.17
  326.6 2.0 copy-start.18
  328.6 176.2 %copy-start.9 = (bf16[1,128,2,256]{3,2,1,0:T(2,128)(2,1)S(1)}, bf16[1,128,2,256]{3,2,1,0:T(2,128)(2,1)}, u32[]{:S(2)}) copy-start(bf16[1,128,2,256]{3,2,1,0:T(2,128)(2,1)} %param.12) | copy-start | bytes 393220
  328.6 176.2 %copy-start.14 = (f32[1,2,256]{2,1,0:T(2,128)S(1)}, f32[1,2,256]{2,1,0:T(2,128)}, u32[]{:S(2)}) copy-start(f32[1,2,256]{2,1,0:T(2,128)} %param.11) | copy-start | bytes 6148
  330.3 179.4 %copy-start.15 = (pred[5]{0:T(512)(128)(4,1)}, pred[5]{0:T(512)(128)(4,1)S(1)}, u32[]{:S(2)}) copy-start(pred[5]{0:T(512)(128)(4,1)S(1)} %fusion.40) | copy-start | bytes 19
  330.9 0.6 copy-start.2
  506.5 0.7 copy-start.5
  509.7 87.1 %copy-start.3 = (s32[5,128,8]{1,2,0:T(8,128)S(1)}, s32[5,128,8]{1,2,0:T(8,128)}, u32[]{:S(2)}) copy-start(s32[5,128,8]{1,2,0:T(8,128)} %copy-done.2) | copy-start | bytes 61444
  509.7 87.1 %copy-start.13 = (pred[5]{0:T(512)(128)(4,1)S(1)}, pred[5]{0:T(512)(128)(4,1)}, u32[]{:S(2)}) copy-start(pred[5]{0:T(512)(128)(4,1)} %compare_and_fusion.2) | copy-start | bytes 19
  509.7 87.2 %copy-start.21 = (s32[5]{0:T(128)S(1)}, s32[5]{0:T(128)}, u32[]{:S(2)}) copy-start(s32[5]{0:T(128)} %compare_select_fusion.7) | copy-start | bytes 64
  509.7 166.7 %copy-start.11 = (pred[128,4,8]{0,1,2:T(4,128)(4,1)S(1)}, pred[128,4,8]{0,1,2:T(4,128)(4,1)}, u32[]{:S(2)}) copy-start(pred[128,4,8]{0,1,2:T(4,128)(4,1)} %get-tuple-element.22) | copy-start | bytes 12292
  676.8 34.5 %copy-start.8 = (bf16[128,4,128]{2,1,0:T(4,128)(2,1)S(1)}, bf16[128,4,128]{2,1,0:T(4,128)(2,1)}, u32[]{:S(2)}) copy-start(bf16[128,4,128]{2,1,0:T(4,128)(2,1)} %param.7) | copy-start | bytes 393220
  708.8 5.7 copy-start.4
  708.8 5.7 copy-start.6
  708.8 5.7 copy-start.16
Sparse Core Ops, SparseCore 0:
  330.4 174.3 all-reduce.1
where the time goes:
time: 732 us; the launch traced here: 728 us
  local copies, waits for them, and re-layouts  297 us (41%)
  waiting for transfers between devices  172 us (23%)
  blocking collectives  161 us (22%)
  other arithmetic  68.5 us (9%)
  matrix products  14.9 us (2%)
  between operations  14.5 us (2%)
    psum x1, waiting for transfers between devices, body(): lax.psum(jnp.einsum('tkf,kc->tcf', per_block, slot_weight, precision=lax....  172 us
    gather x6, local copies, waits for them, and re-layouts, pick_rows(): return jnp.take(weight_table, row_index, axis=0)  156 us
    gather x5, local copies, waits for them, and re-layouts, body(): per_block = jnp.take_along_axis(dense_grad, picked_source, axis=2)  87.4 us
    psum x1, blocking collectives, body(): pre_total = lax.psum(partial_value, 'layer')  81.2 us
    psum x1, blocking collectives, body(): lax.psum(jnp.einsum('tks,kl->tls', per_block, source_onehot, precision=la...  79.4 us
    unnamed x5, other arithmetic  59.8 us
    gather x5, local copies, waits for them, and re-layouts, body(): jnp.take_along_axis(jnp.where(inside, local_index, 0), position, axis=2)  34 us
  transfers between devices with their start and end apart: 1, of which 1 were waited for; matrix products, arithmetic and copies ran while one was open for 0% of the time, Pallas kernels for 0%

commit v1 on v0

--- a/solution.py
+++ b/solution.py
@@ -56,8 +56,12 @@
     per_block = jnp.einsum(
         "tks,ksf->tkf", act_source, decoder_own, preferred_element_type=jnp.float32
     )
-    rebuilt = lax.psum(
-        jnp.einsum("tkf,kc->tcf", per_block, slot_weight, precision=lax.Precision.HIGHEST), "lat"
+    rebuilt = jnp.sum(
+        lax.all_gather(
+            jnp.einsum("tkf,kc->tcf", per_block, slot_weight, precision=lax.Precision.HIGHEST),
+            "lat",
+        ),
+        axis=0,
     )
     residue = (rebuilt + dec_bias[0][None, :, :] - targets[0].astype(jnp.float32)).astype(
         jnp.bfloat16

time: 732 us -> 636 us (0.87)
  waiting for transfers between devices: 172 us -> 73.7 us
    psum x1 -> x0, waiting for transfers between devices: 172 us -> none  [body(): lax.psum(jnp.einsum('tkf,kc->tcf', per_block, slot_weight, precision=lax....]
    all_gather x0 -> x1, waiting for transfers between devices: none -> 73.7 us  [body(): lax.all_gather(jnp.einsum('tkf,kc->tcf', per_block, slot_weight, precisio...]
where the time goes in v1:
time: 636 us; the launch traced here: 631 us
  local copies, waits for them, and re-layouts  297 us (47%)
  blocking collectives  160 us (25%)
  waiting for transfers between devices  73.7 us (12%)
  other arithmetic  71.1 us (11%)
  matrix products  14.9 us (2%)
  between operations  14.5 us (2%)
    gather x6, local copies, waits for them, and re-layouts, pick_rows(): return jnp.take(weight_table, row_index, axis=0)  156 us
    gather x5, local copies, waits for them, and re-layouts, body(): per_block = jnp.take_along_axis(dense_grad, picked_source, axis=2)  87.4 us
    psum x1, blocking collectives, body(): pre_total = lax.psum(partial_value, 'layer')  81.2 us
    psum x1, blocking collectives, body(): lax.psum(jnp.einsum('tks,kl->tls', per_block, source_onehot, precision=la...  79.3 us
    all_gather x1, waiting for transfers between devices, body(): lax.all_gather(jnp.einsum('tkf,kc->tcf', per_block, slot_weight, precisio...  73.7 us
    unnamed x5, other arithmetic  59.8 us
    gather x5, local copies, waits for them, and re-layouts, body(): jnp.take_along_axis(jnp.where(inside, local_index, 0), position, axis=2)  34 us
  transfers between devices with their start and end apart: 1, of which 1 were waited for; matrix products, arithmetic and copies ran while one was open for 0% of the time, Pallas kernels for 0%

profile of v1, /device:TPU:6, one launch (start us, length us, event | category | flops | bytes accessed | tf_op | source)
XLA Modules:
  0.0 631.3 jit_solution(10442366458464503281)
XLA Ops:
  7.2 0.5 compare_and_fusion.2
  7.8 0.6 iota_compare_fusion.1
  8.4 0.9 iota_subtract_fusion
  9.3 1.7 top_k.12
  11.5 33.2 %gather_fusion.3 = s32[4096]{0:T(1024)S(1)} fusion(s32[128,4,64]{0,2,1:T(8,128)S(1)} %get-tuple-element.26, s32[4096]{0:T(1024)S(1)} %reshape.136), kind=kCustom, calls=%fused_computation.3 | custom fusion | bytes 81920 | tf_op jit(solution)/shard_map/jit(take_along_axis)/gather | solution.py:27
  46.1 34.9 %gather_fusion.5 = f32[4096]{0:T(1024)S(1)} fusion(f32[4,1024]{1,0:T(4,128)S(1)} %copy-done.1, s32[4096]{0:T(1024)S(1)} %reshape.142), kind=kCustom, calls=%fused_computation.5 | custom fusion | bytes 65536 | tf_op jit(solution)/shard_map/vmap(jit(_take))/gather | solution.py:10
  81.7 2.3 copy.62
  84.0 120.8 %gather_fusion.4 = bf16[4096,128]{1,0:T(8,128)(2,1)} fusion(bf16[4,1024,128]{2,1,0:T(8,128)(2,1)} %bitcast.89, s32[4096]{0:T(1024)S(1)} %reshape.142), kind=kCustom, calls=%fused_computation.4 | custom fusion | bytes 2129920 | tf_op jit(solution)/shard_map/vmap(jit(_take))/gather | solution.py:10
  204.9 2.1 fusion.16
  207.1 81.2 %psum.14 = f32[128,4,8]{0,1,2:T(4,128)S(1)} all-reduce(f32[128,4,8]{0,1,2:T(4,128)S(1)} %bitcast.93), channel_id=1, replica_groups=mesh['layer'=16,'lat'=16] {'layer'}, use_global_device_ids=true, to_apply=%region_1.2 | all-reduce | flops 4096 | bytes 32768 | tf_op jit(solution)/shard_map/psum | solution.py:31
  288.3 0.6 fusion.33
  289.2 29.7 %scatter_custom_fusion = bf16[524288]{0:T(1024)(128)(2,1)} fusion(s32[4096]{0:T(1024)S(1)} %reshape.160, bf16[4096]{0:T(1024)(128)(2,1)S(1)} %reshape.162, bf16[]{:T(256)} %constant.131.clone.1), kind=kCustom, calls=%fused_computation.30 | custom fusion | flops 4096 | bytes 1048578
  319.0 2.1 reshape.106
  321.1 2.5 copy.66
  323.6 3.0 gather_fusion
  326.6 1.9 fusion.9
  328.6 1.7 convolution_bitcast_fusion.2
  330.3 0.6 gather_fusion.2
  331.9 0.6 compare_select_fusion.7
  332.5 73.7 %all-gather.3.cloned.1.call-done = f32[2048,2,256]{2,1,0:T(2,128)} async-done(((f32[128,2,256]{2,1,0:T(2,128)}), f32[2048,2,256]{2,1,0:T(2,128)}) %all-gather.3.cloned.1.call-update) | async-done | bytes 4194320 | tf_op jit(solution)/shard_map/all_gather | solution.py:60
  406.1 3.6 reduce_sum.18
  409.8 0.6 gather_fusion.1
  410.4 0.7 copy-done.5
  411.1 2.5 fusion.4
  413.6 86.8 %gather_fusion.6 = f32[5120]{0:T(1024)S(1)} fusion(f32[128,5,1024]{2,0,1:T(8,128)} %fusion.4, s32[5120]{0:T(1024)S(1)} %reshape.154), kind=kCustom, calls=%fused_computation.6 | custom fusion | bytes 102400 | tf_op jit(solution)/shard_map/jit(take_along_axis)/gather | solution.py:77
  500.9 79.3 %psum.15 = bf16[128,4,8]{0,1,2:T(4,128)(2,1)S(1)} all-reduce(f32[128,4,8]{0,1,2:T(4,128)S(1)} %convolution_bitcast_fusion.3), channel_id=1, replica_groups=mesh['layer'=16,'lat'=16] {'layer'}, use_global_device_ids=true, to_apply=%region_4.5 | all-reduce | flops 4096 | bytes 24576 | tf_op jit(solution)/shard_map/psum | solution.py:78
  580.5 29.9 %scatter_custom_fusion.1 = bf16[524288]{0:T(1024)(128)(2,1)} fusion(s32[4096]{0:T(1024)} %copy-done.10, bf16[4096]{0:T(1024)(128)(2,1)S(1)} %reshape.168, bf16[]{:T(256)} %constant.131.clone.1), kind=kCustom, calls=%fused_computation.28 | custom fusion | flops 4096 | bytes 1049088
  610.4 2.2 reshape.110
  612.6 2.4 convert_reduce_fusion
  615.0 3.2 convolution_bitcast_fusion.1
  618.2 3.4 convolution_bitcast_fusion
  621.6 2.9 copy.78
  (88 shorter events, 4.9 us)
Async XLA Ops:
  7.2 319.5 %copy-start = (bf16[1,5,1024,256]{3,2,1,0:T(8,128)(2,1)S(1)}, bf16[1,5,1024,256]{3,2,1,0:T(8,128)(2,1)}, u32[]{:S(2)}) copy-start(bf16[1,5,1024,256]{3,2,1,0:T(8,128)(2,1)} %param.10) | copy-start | bytes 7864324
  7.2 399.0 %all-gather.3.cloned.1.call-start = ((), (), s32[]{:S(2)}) async-start(), calls=%async_computation | async-start | bytes 4456448 | tf_op jit(solution)/shard_map/all_gather | solution.py:60
  11.5 33.9 %copy-start.20 = (s32[3]{0:T(128)S(1)}, s32[3]{0:T(128)}, u32[]{:S(2)}) copy-start(s32[3]{0:T(128)} %constant.147) | copy-start | bytes 40
  11.5 34.0 %copy-start.19 = (s32[3]{0:T(128)S(1)}, s32[3]{0:T(128)}, u32[]{:S(2)}) copy-start(s32[3]{0:T(128)} %constant.144) | copy-start | bytes 40
  44.8 1.4 copy-start.1
  81.7 207.5 %copy-start.10 = (s32[4096]{0:T(1024)}, s32[4096]{0:T(1024)S(1)}, u32[]{:S(2)}) copy-start(s32[4096]{0:T(1024)S(1)} %reshape.160) | copy-start | bytes 49156
  84.0 120.8 %copy-start.7 = (bf16[128,4,128]{2,1,0:T(4,128)(2,1)S(1)}, bf16[128,4,128]{2,1,0:T(4,128)(2,1)}, u32[]{:S(2)}) copy-start(bf16[128,4,128]{2,1,0:T(4,128)(2,1)} %param.7) | copy-start | bytes 393220
  323.6 3.0 copy-start.12
  326.6 2.0 copy-start.17
  326.6 2.0 copy-start.18
  330.8 0.6 copy-start.2
  331.9 78.5 %copy-start.15 = (pred[5]{0:T(512)(128)(4,1)}, pred[5]{0:T(512)(128)(4,1)S(1)}, u32[]{:S(2)}) copy-start(pred[5]{0:T(512)(128)(4,1)S(1)} %fusion.40) | copy-start | bytes 19
  406.1 3.6 copy-start.9
  406.1 3.6 copy-start.14
  410.4 0.7 copy-start.5
  413.6 87.1 %copy-start.3 = (s32[5,128,8]{1,2,0:T(8,128)S(1)}, s32[5,128,8]{1,2,0:T(8,128)}, u32[]{:S(2)}) copy-start(s32[5,128,8]{1,2,0:T(8,128)} %copy-done.2) | copy-start | bytes 61444
  413.6 87.1 %copy-start.13 = (pred[5]{0:T(512)(128)(4,1)S(1)}, pred[5]{0:T(512)(128)(4,1)}, u32[]{:S(2)}) copy-start(pred[5]{0:T(512)(128)(4,1)} %compare_and_fusion.2) | copy-start | bytes 19
  413.6 87.2 %copy-start.21 = (s32[5]{0:T(128)S(1)}, s32[5]{0:T(128)}, u32[]{:S(2)}) copy-start(s32[5]{0:T(128)} %compare_select_fusion.7) | copy-start | bytes 64
  413.6 166.6 %copy-start.11 = (pred[128,4,8]{0,1,2:T(4,128)(4,1)S(1)}, pred[128,4,8]{0,1,2:T(4,128)(4,1)}, u32[]{:S(2)}) copy-start(pred[128,4,8]{0,1,2:T(4,128)(4,1)} %get-tuple-element.22) | copy-start | bytes 12292
  580.5 34.5 %copy-start.8 = (bf16[128,4,128]{2,1,0:T(4,128)(2,1)S(1)}, bf16[128,4,128]{2,1,0:T(4,128)(2,1)}, u32[]{:S(2)}) copy-start(bf16[128,4,128]{2,1,0:T(4,128)(2,1)} %param.7) | copy-start | bytes 393220
  612.6 5.7 copy-start.4
  612.6 5.7 copy-start.6
  612.6 5.7 copy-start.16
Sparse Core Ops, SparseCore 0:
  330.4 75.7 all-gather.2
